TPU v7x, 128 devices: a whole 4x4x4 slice. The times are simulated.
128 devices in a mesh: seq: 32 (over z, x, core), batch: 4 (over y).
Axes of the slice: x: 4, y: 4, z: 4, core: 2. Of those that a mesh axis runs over, the one named last changes fastest.
Arguments:
- sequence_input: bfloat16 [32768, 1536], P(('batch', 'seq')), parts along dimension 0, may hold values from -6 to 6
- conv_first: bfloat16 [5, 1536, 768], replicated, may hold values from -0.0625 to 0.0625
- conv_second: bfloat16 [5, 768, 768], replicated, may hold values from -0.09375 to 0.09375
- qkv_weight: bfloat16 [768, 1536], replicated, may hold values from -0.21875 to 0.21875
- out_weight: bfloat16 [512, 768], replicated, may hold values from -0.25 to 0.25
- logit_scale: float32 [4], replicated, may hold values from 2.5 to 30, as said below
Outputs:
- block_output: bfloat16 [32768, 768], P(('batch', 'seq')), parts along dimension 0
There are 4 independent parts, one for each index of `batch`. A program takes and returns all parts, laid end to end along the dimension named above; an argument that names none is the same for every part. Nothing has to cross between parts.
Inputs may be any that keep to these rules, and one draw needn't show every extreme that they name: `logit_scale`: one positive scale a head.
All inputs are finite; a program needn't handle non-finite values.
Results may differ from a plain program's by a relative error of at most 0.023.
Values may be sent and summed in bfloat16 or wider, within the bound.
A program may use at most 256 MiB of HBM per device.

v0:
```python
import math
import jax
import jax.numpy as jnp
from jax import lax
from jax.sharding import PartitionSpec as P


def padded_2(block, sides, width):
    for axis, dim in sides:
        count = lax.axis_size(axis)
        forward = [(i, i + 1) for i in range(count - 1)]
        backward = [(target, source) for source, target in forward]
        low = lax.ppermute(
            lax.slice_in_dim(block, block.shape[dim] - width, None, axis=dim), axis, forward
        )
        high = lax.ppermute(lax.slice_in_dim(block, 0, width, axis=dim), axis, backward)
        block = jnp.concatenate([low, block, high], axis=dim)
    return block


def convolve(padded, weight, row_count):
    conv_sum = jnp.dot(padded[0:row_count], weight[0], preferred_element_type=jnp.float32)
    for offset in range(1, weight.shape[0]):
        conv_sum = conv_sum + jnp.dot(
            padded[offset : offset + row_count], weight[offset], preferred_element_type=jnp.float32
        )
    return conv_sum


def head_rms(tensor):
    return tensor * lax.rsqrt(jnp.mean(tensor * tensor, axis=-1, keepdims=True) + 1e-06)


def attend_block(state_now, queries, key_block, value_block):
    running_max, running_sum, running_out = state_now
    scores = jnp.einsum("thd,shd->hts", queries, key_block, preferred_element_type=jnp.float32)
    new_max = jnp.maximum(running_max, jnp.max(scores, axis=2))
    weights = jnp.exp(scores - new_max[:, :, None])
    running_sum = jnp.sum(weights, axis=2)
    running_out = jnp.einsum(
        "hts,shd->htd",
        weights.astype(jnp.bfloat16),
        value_block,
        preferred_element_type=jnp.float32,
    )
    return (new_max, running_sum, running_out)


def body(sequence_input, conv_first, conv_second, qkv_weight, out_weight, logit_scale):
    row_count = sequence_input.shape[0]
    padded_input = padded_2(sequence_input, (("seq", 0),), 2)
    first_out = jax.nn.gelu(convolve(padded_input, conv_first, row_count)).astype(jnp.bfloat16)
    padded_first = padded_2(first_out, (("seq", 0),), 2)
    second = convolve(padded_first, conv_second, row_count)
    hidden = (first_out.astype(jnp.float32) + second).astype(jnp.bfloat16)
    head_count = logit_scale.shape[0]
    width_all = qkv_weight.shape[1] // 3
    head_size = width_all // head_count
    query_part = jnp.dot(hidden, qkv_weight[:, :width_all], preferred_element_type=jnp.float32)
    query_part = query_part.reshape(row_count, head_count, head_size)
    queries = (head_rms(query_part) * (logit_scale / math.sqrt(head_size))[None, :, None]).astype(
        jnp.bfloat16
    )
    kv_weight = qkv_weight[:, width_all:]
    start_state = (
        jnp.full((head_count, row_count), -1e30, jnp.float32),
        jnp.zeros((head_count, row_count), jnp.float32),
        jnp.zeros((head_count, row_count, head_size), jnp.float32),
    )
    piece_rows = hidden.shape[0]
    paired = jnp.dot(hidden, kv_weight, preferred_element_type=jnp.float32)
    key_block = head_rms(paired[:, :width_all].reshape(piece_rows, head_count, head_size)).astype(
        jnp.bfloat16
    )
    value_block = (
        paired[:, width_all:].reshape(piece_rows, head_count, head_size).astype(jnp.bfloat16)
    )
    own_keys = key_block
    own_values = value_block
    flat_keys = own_keys.reshape(row_count, width_all)
    flat_values = own_values.reshape(row_count, width_all)
    piece_pair = (
        lax.all_gather(flat_keys, "seq", axis=0, tiled=True),
        lax.all_gather(flat_values, "seq", axis=0, tiled=True),
    )
    piece_rows = piece_pair[0].shape[0]
    key_block = piece_pair[0].reshape(piece_rows, head_count, head_size)
    value_block = piece_pair[1].reshape(piece_rows, head_count, head_size)
    final_state = attend_block(start_state, queries, key_block, value_block)
    running_max, running_sum, running_out = final_state
    attended = (
        (running_out / running_sum[:, :, None])
        .transpose(1, 0, 2)
        .reshape(row_count, width_all)
        .astype(jnp.bfloat16)
    )
    return (
        hidden.astype(jnp.float32)
        + jnp.dot(attended, out_weight, preferred_element_type=jnp.float32)
    ).astype(jnp.bfloat16)


def solution(mesh):
    in_specs = (P(("batch", "seq"), None), P(), P(), P(), P(), P())
    out_specs = P(("batch", "seq"), None)
    return jax.shard_map(body, mesh=mesh, in_specs=in_specs, out_specs=out_specs, check_vma=False)
```

profile of v0, /device:TPU:1, one launch (start us, length us, event | category | flops | bytes accessed | tf_op | source)
XLA Modules:
  0.0 185.4 jit_solution(1731052009252895028)
XLA Ops:
  6.5 0.8 fusion.101
  7.4 3.3 %collective-permute-start.1 = (bf16[2,1536]{1,0:T(2,128)(2,1)S(1)}, bf16[2,1536]{1,0:T(2,128)(2,1)S(1)}, u32[]{:S(2)}, u32[]{:S(2)}) collective-permute-start(bf16[2,1536]{1,0:T(2,128)(2,1)S(1)} %get-tuple-element.6), channel_id=1, source_target_pairs={{4,0},{8,4},{12,8},{16,12},{20,16},{24,20},{28,24},{32,28},{36,32}... | collective-permute-start | bytes 18440 | tf_op jit(solution)/shard_map/ppermute | solution.py:16
  10.7 3.5 %collective-permute-start = (bf16[2,1536]{1,0:T(2,128)(2,1)S(1)}, bf16[2,1536]{1,0:T(2,128)(2,1)S(1)}, u32[]{:S(2)}, u32[]{:S(2)}) collective-permute-start(bf16[2,1536]{1,0:T(2,128)(2,1)S(1)} %get-tuple-element.5), channel_id=1, source_target_pairs={{0,4},{4,8},{8,12},{12,16},{16,20},{20,24},{24,28},{28,32},{32,36}... | collective-permute-start | bytes 18440 | tf_op jit(solution)/shard_map/ppermute | solution.py:13
  14.2 2.7 %fusion.12 = f32[256,768]{1,0:T(8,128)S(1)} fusion(bf16[256,1536]{1,0:T(8,128)(2,1)} %param.6, bf16[5,1536,768]{2,1,0:T(8,128)(2,1)} %param.7), kind=kOutput, calls=%fused_computation.12 | convolution fusion | flops 603979776 | bytes 3932160 | tf_op jit(solution)/shard_map/dot_general | solution.py:24
  16.9 1.2 constant_dynamic-update-slice_fusion.1
  18.2 2.5 %fusion.8 = f32[256,768]{1,0:T(8,128)S(1)} fusion(bf16[5,1536,768]{2,1,0:T(8,128)(2,1)} %param.7, bf16[258,1536]{1,0:T(8,128)(2,1)S(1)} %constant_dynamic-update-slice_fusion), kind=kOutput, calls=%fused_computation.8 | convolution fusion | flops 603979776 | bytes 3932160 | tf_op jit(solution)/shard_map/dot_general | solution.py:24
  20.7 0.8 fusion.10
  21.5 0.8 fusion.14
  22.4 1.0 fusion.77
  23.4 2.9 %collective-permute-start.2 = (bf16[2,768]{1,0:T(2,128)(2,1)S(1)}, bf16[2,768]{1,0:T(2,128)(2,1)S(1)}, u32[]{:S(2)}, u32[]{:S(2)}) collective-permute-start(bf16[2,768]{1,0:T(2,128)(2,1)S(1)} %get-tuple-element.7), channel_id=1, source_target_pairs={{0,4},{4,8},{8,12},{12,16},{16,20},{20,24},{24,28},{28,32},{32,36}... | collective-permute-start | bytes 9224 | tf_op jit(solution)/shard_map/ppermute | solution.py:13
  26.8 1.9 %collective-permute-start.3 = (bf16[2,768]{1,0:T(2,128)(2,1)S(1)}, bf16[2,768]{1,0:T(2,128)(2,1)S(1)}, u32[]{:S(2)}, u32[]{:S(2)}) collective-permute-start(bf16[2,768]{1,0:T(2,128)(2,1)S(1)} %get-tuple-element.8), channel_id=1, source_target_pairs={{4,0},{8,4},{12,8},{16,12},{20,16},{24,20},{28,24},{32,28},{36,32}... | collective-permute-start | bytes 9224 | tf_op jit(solution)/shard_map/ppermute | solution.py:16
  29.3 2.5 %collective-permute-done.3 = bf16[2,768]{1,0:T(2,128)(2,1)S(1)} collective-permute-done((bf16[2,768]{1,0:T(2,128)(2,1)S(1)}, bf16[2,768]{1,0:T(2,128)(2,1)S(1)}, u32[]{:S(2)}, u32[]{:S(2)}) %collective-permute-start.3) | collective-permute-done | bytes 3104 | tf_op jit(solution)/shard_map/ppermute | solution.py:16
  32.8 0.5 fusion.40
  33.3 0.6 fusion.23
  34.9 0.8 fusion.87
  35.9 0.7 slice.220
  36.7 1.5 fusion.85
  39.1 55.5 %all-gather.3.cloned.1.call-done = bf16[8192,512]{1,0:T(8,128)(2,1)} async-done(((bf16[256,512]{1,0:T(8,128)(2,1)}), bf16[8192,512]{1,0:T(8,128)(2,1)}) %all-gather.3.cloned.1.call-update) | async-done | bytes 8388624 | tf_op jit(solution)/shard_map/all_gather | solution.py:83
  94.6 16.8 %fusion.103 = (f32[4,256]{1,0:T(4,128)S(1)}, f32[4,256,8192]{2,1,0:T(8,128)}) fusion(bf16[256,4,128]{2,1,0:T(4,128)(2,1)S(1)} %multiply_convert_fusion, bf16[8192,512]{1,0:T(8,128)(2,1)} %all-gather.3.cloned.1.call-done), kind=kOutput, calls=%fused_computation.102 | convolution fusion | flops 2155871232 | bytes 42209280 | tf_op jit(solution)/shard_map/thd,shd->hts/dot_general | solution.py:36
  111.4 13.7 %fusion = f32[4,256]{1,0:T(4,128)S(1)} fusion(f32[4,256,8192]{2,1,0:T(8,128)} %get-tuple-element.10, f32[4,256]{1,0:T(4,128)S(1)} %broadcast_maximum_fusion), kind=kLoop, calls=%fused_computation.1 | loop fusion | flops 16776192 | bytes 33562624 | tf_op jit(solution)/shard_map/reduce_sum | solution.py:39
  125.2 24.3 %all-gather.5.cloned.1.call-done = bf16[8192,512]{1,0:T(8,128)(2,1)} async-done(((bf16[256,512]{1,0:T(8,128)(2,1)}), bf16[8192,512]{1,0:T(8,128)(2,1)}) %all-gather.5.cloned.1.call-update) | async-done | bytes 8388624 | tf_op jit(solution)/shard_map/all_gather | solution.py:84
  149.4 12.0 %copy.21 = bf16[8192,512]{0,1:T(8,128)(2,1)} copy(bf16[8192,512]{1,0:T(8,128)(2,1)} %all-gather.5.cloned.1.call-done) | data formatting | bytes 16777216 | tf_op jit(solution)/shard_map/reshape | solution.py:88
  161.4 16.0 %fusion.48 = bf16[256,4,128]{0,2,1:T(8,128)(2,1)S(1)} fusion(bf16[8192,4,128]{0,2,1:T(8,128)(2,1)} %bitcast.72, f32[4,256,8192]{2,1,0:T(8,128)} %get-tuple-element.10, f32[4,256]{1,0:T(4,128)S(1)} %broadcast_maximum_fusion, f32[256,4]{0,1:T(4,128)S(1)} %bitcast.77), kind=kOutput, calls=%fused_computation.39 | convolution fusion | flops 2164523008 | bytes 42213376 | tf_op jit(solution)/shard_map/hts,shd->htd/dot_general | solution.py:40
  177.5 1.1 fusion.41
  (39 shorter events, 4.1 us)
Async XLA Ops:
  6.5 170.9 %copy-start = (bf16[512,768]{1,0:T(8,128)(2,1)S(1)}, bf16[512,768]{1,0:T(8,128)(2,1)}, u32[]{:S(2)}) copy-start(bf16[512,768]{1,0:T(8,128)(2,1)} %param.10) | copy-start | bytes 2359300
  6.5 88.1 %all-gather.3.cloned.1.call-start = ((), (), s32[]{:S(2)}) async-start(), calls=%async_computation | async-start | bytes 8650752 | tf_op jit(solution)/shard_map/all_gather | solution.py:83
  7.4 10.8 %collective-permute-start.1 = (bf16[2,1536]{1,0:T(2,128)(2,1)S(1)}, bf16[2,1536]{1,0:T(2,128)(2,1)S(1)}, u32[]{:S(2)}, u32[]{:S(2)}) collective-permute-start(bf16[2,1536]{1,0:T(2,128)(2,1)S(1)} %get-tuple-element.6), channel_id=1, source_target_pairs={{4,0},{8,4},{12,8},{16,12},{20,16},{24,20},{28,24},{32,28},{36,32}... | collective-permute-start | bytes 18440 | tf_op jit(solution)/shard_map/ppermute | solution.py:16
  10.7 10.0 %copy-start.3 = (bf16[5,1536,768]{2,1,0:T(8,128)(2,1)S(1)}, bf16[5,1536,768]{2,1,0:T(8,128)(2,1)}, u32[]{:S(2)}) copy-start(bf16[5,1536,768]{2,1,0:T(8,128)(2,1)} %param.7) | copy-start | bytes 35389444
  10.7 10.8 %collective-permute-start = (bf16[2,1536]{1,0:T(2,128)(2,1)S(1)}, bf16[2,1536]{1,0:T(2,128)(2,1)S(1)}, u32[]{:S(2)}, u32[]{:S(2)}) collective-permute-start(bf16[2,1536]{1,0:T(2,128)(2,1)S(1)} %get-tuple-element.5), channel_id=1, source_target_pairs={{0,4},{4,8},{8,12},{12,16},{16,20},{20,24},{24,28},{28,32},{32,36}... | collective-permute-start | bytes 18440 | tf_op jit(solution)/shard_map/ppermute | solution.py:13
  18.1 3.4 %copy-start.2 = (bf16[256,1536]{1,0:T(8,128)(2,1)S(1)}, bf16[256,1536]{1,0:T(8,128)(2,1)}, u32[]{:S(2)}) copy-start(bf16[256,1536]{1,0:T(8,128)(2,1)} %param.6) | copy-start | bytes 2359300
  21.5 4.8 %slice-start = ((s8[5898240]{0:T(1024)(128)(4,1)}), s8[4194304]{0:T(1024)(128)(4,1)S(1)}, s32[]{:S(2)}) async-start(s8[5898240]{0:T(1024)(128)(4,1)} %bitcast.73), calls=%async_computation.2 | async-start | bytes 8388608
  22.4 4.0 %slice-start.1 = ((s8[5898240]{0:T(1024)(128)(4,1)}), s8[1703936]{0:T(1024)(128)(4,1)S(1)}, s32[]{:S(2)}) async-start(s8[5898240]{0:T(1024)(128)(4,1)} %bitcast.73), calls=%async_computation.3 | async-start | bytes 3407872
  23.4 5.4 %collective-permute-start.2 = (bf16[2,768]{1,0:T(2,128)(2,1)S(1)}, bf16[2,768]{1,0:T(2,128)(2,1)S(1)}, u32[]{:S(2)}, u32[]{:S(2)}) collective-permute-start(bf16[2,768]{1,0:T(2,128)(2,1)S(1)} %get-tuple-element.7), channel_id=1, source_target_pairs={{0,4},{4,8},{8,12},{12,16},{16,20},{20,24},{24,28},{28,32},{32,36}... | collective-permute-start | bytes 9224 | tf_op jit(solution)/shard_map/ppermute | solution.py:13
  26.8 4.9 %collective-permute-start.3 = (bf16[2,768]{1,0:T(2,128)(2,1)S(1)}, bf16[2,768]{1,0:T(2,128)(2,1)S(1)}, u32[]{:S(2)}, u32[]{:S(2)}) collective-permute-start(bf16[2,768]{1,0:T(2,128)(2,1)S(1)} %get-tuple-element.8), channel_id=1, source_target_pairs={{4,0},{8,4},{12,8},{16,12},{20,16},{24,20},{28,24},{32,28},{36,32}... | collective-permute-start | bytes 9224 | tf_op jit(solution)/shard_map/ppermute | solution.py:16
  29.3 4.0 %copy-start.1 = (bf16[768,1536]{1,0:T(8,128)(2,1)S(1)}, bf16[768,1536]{1,0:T(8,128)(2,1)}, u32[]{:S(2)}) copy-start(bf16[768,1536]{1,0:T(8,128)(2,1)} %param.9) | copy-start | bytes 7077892
  32.8 3.9 %copy-start.4 = (f32[4]{0:T(128)S(1)}, f32[4]{0:T(128)}, u32[]{:S(2)}) copy-start(f32[4]{0:T(128)} %param.11) | copy-start | bytes 52
  35.7 113.8 %all-gather.5.cloned.1.call-start = ((), (), s32[]{:S(2)}) async-start(), calls=%async_computation.1 | async-start | bytes 8650752 | tf_op jit(solution)/shard_map/all_gather | solution.py:84
Sparse Core Ops, SparseCore 0:
  35.8 58.7 all-gather.2
  96.9 52.5 all-gather.4
where the time goes:
time: 186 us; the launch traced here: 185 us
  waiting for transfers between devices  82.3 us (44%)
  matrix products  46.4 us (25%)
  other arithmetic  15.6 us (8%)
  local copies, waits for them, and re-layouts  15.5 us (8%)
  between operations  13.8 us (7%)
  starting transfers between devices  11.9 us (6%)
    all_gather x1, waiting for transfers between devices, body(): lax.all_gather(flat_keys, 'seq', axis=0, tiled=True)  55.5 us
    all_gather x1, waiting for transfers between devices, body(): lax.all_gather(flat_values, 'seq', axis=0, tiled=True)  24.3 us
    dot_general x1, matrix products, attend_block(): jnp.einsum('thd,shd->hts', queries, key_block, preferred_element_type=jnp...  16.8 us
    dot_general x1, matrix products, attend_block(): jnp.einsum('hts,shd->htd', weights.astype(jnp.bfloat16), value_block, pre...  16 us
    reduce_sum x1, other arithmetic, attend_block(): running_sum = jnp.sum(weights, axis=2)  13.7 us
    reshape x1, local copies, waits for them, and re-layouts, body(): value_block = piece_pair[1].reshape(piece_rows, head_count, head_size)  12 us
    dot_general x8, matrix products, convolve(): jnp.dot(padded[offset:offset + row_count], weight[offset], preferred_elem...  8.8 us
    ppermute x2, starting transfers between devices, padded_2(): lax.ppermute(lax.slice_in_dim(block, block.shape[dim] - width, None, axis...  6.42 us
  transfers between devices with their start and end apart: 6, of which 3 were waited for; matrix products, arithmetic and copies ran while one was open for 23% of the time, Pallas kernels for 0%

commit v1 on v0

--- a/solution.py
+++ b/solution.py
@@ -80,7 +80,9 @@
     flat_keys = own_keys.reshape(row_count, width_all)
     flat_values = own_values.reshape(row_count, width_all)
     piece_pair = (
-        lax.all_gather(flat_keys, "seq", axis=0, tiled=True),
+        jnp.concatenate(
+            lax.all_to_all(jnp.stack([flat_keys] * lax.axis_size("seq")), "seq", 0, 0), axis=0
+        ),
         lax.all_gather(flat_values, "seq", axis=0, tiled=True),
     )
     piece_rows = piece_pair[0].shape[0]

time: 186 us -> 263 us (1.41)
  the two profiles are of different devices: /device:TPU:1 before, /device:TPU:0 now
where the time goes in v1:
time: 263 us; the launch traced here: 262 us
  waiting for transfers between devices  120 us (46%)
  matrix products  46.1 us (18%)
  local copies, waits for them, and re-layouts  44.7 us (17%)
  starting transfers between devices  23.2 us (9%)
  other arithmetic  14.9 us (6%)
  between operations  13.8 us (5%)
    all_to_all x1, waiting for transfers between devices, body(): lax.all_to_all(jnp.stack([flat_keys] * lax.axis_size('seq')), 'seq', 0, 0)  118 us
    dot_general x1, matrix products, attend_block(): jnp.einsum('thd,shd->hts', queries, key_block, preferred_element_type=jnp...  16.5 us
    dot_general x1, matrix products, attend_block(): jnp.einsum('hts,shd->htd', weights.astype(jnp.bfloat16), value_block, pre...  16 us
    all_to_all x1, starting transfers between devices, body(): lax.all_to_all(jnp.stack([flat_keys] * lax.axis_size('seq')), 'seq', 0, 0)  14.1 us
    reduce_sum x1, other arithmetic, attend_block(): running_sum = jnp.sum(weights, axis=2)  13.6 us
    another operation x1, local copies, waits for them, and re-layouts, body(): key_block = piece_pair[0].reshape(piece_rows, head_count, head_size)  13.4 us
    reshape x1, local copies, waits for them, and re-layouts, body(): value_block = piece_pair[1].reshape(piece_rows, head_count, head_size)  12 us
    all_to_all x1, local copies, waits for them, and re-layouts, body(): lax.all_to_all(jnp.stack([flat_keys] * lax.axis_size('seq')), 'seq', 0, 0)  11.4 us
  transfers between devices with their start and end apart: 6, of which 2 were waited for; matrix products, arithmetic and copies ran while one was open for 27% of the time, Pallas kernels for 0%

profile of v1, /device:TPU:0, one launch (start us, length us, event | category | flops | bytes accessed | tf_op | source)
XLA Modules:
  0.0 262.2 jit_solution(4857593313068001192)
XLA Ops:
  6.5 0.8 fusion.99
  7.4 1.3 collective-permute-start.1
  8.7 3.4 %collective-permute-start = (bf16[2,1536]{1,0:T(2,128)(2,1)S(1)}, bf16[2,1536]{1,0:T(2,128)(2,1)S(1)}, u32[]{:S(2)}, u32[]{:S(2)}) collective-permute-start(bf16[2,1536]{1,0:T(2,128)(2,1)S(1)} %get-tuple-element.5), channel_id=1, source_target_pairs={{0,4},{4,8},{8,12},{12,16},{16,20},{20,24},{24,28},{28,32},{32,36}... | collective-permute-start | bytes 18440 | tf_op jit(solution)/shard_map/ppermute | solution.py:13
  12.1 2.7 %fusion.9 = f32[256,768]{1,0:T(8,128)S(1)} fusion(bf16[256,1536]{1,0:T(8,128)(2,1)} %param.6, bf16[5,1536,768]{2,1,0:T(8,128)(2,1)} %param.7), kind=kOutput, calls=%fused_computation.9 | convolution fusion | flops 603979776 | bytes 3932160 | tf_op jit(solution)/shard_map/dot_general | solution.py:24
  14.8 1.2 constant_dynamic-update-slice_fusion.1
  16.1 2.5 fusion.5
  18.6 0.8 fusion.7
  19.4 0.8 fusion.11
  20.3 1.0 fusion.74
  21.3 3.1 %collective-permute-start.2 = (bf16[2,768]{1,0:T(2,128)(2,1)S(1)}, bf16[2,768]{1,0:T(2,128)(2,1)S(1)}, u32[]{:S(2)}, u32[]{:S(2)}) collective-permute-start(bf16[2,768]{1,0:T(2,128)(2,1)S(1)} %get-tuple-element.7), channel_id=1, source_target_pairs={{0,4},{4,8},{8,12},{12,16},{16,20},{20,24},{24,28},{28,32},{32,36}... | collective-permute-start | bytes 9224 | tf_op jit(solution)/shard_map/ppermute | solution.py:13
  24.9 1.3 collective-permute-start.3
  26.7 1.8 collective-permute-done.3
  30.6 0.7 slice.220
  32.6 4.2 %stack.3 = bf16[32,256,512]{1,2,0:T(8,128)(2,1)} broadcast(bf16[256,512]{0,1:T(8,128)(2,1)S(1)} %copy.24), dimensions={1,2} | broadcast | bytes 8650752 | tf_op jit(solution)/shard_map/stack | solution.py:84
  36.7 14.1 %all-to-all-start = ((bf16[32,256,512]{1,2,0:T(8,128)(2,1)}), bf16[32,256,512]{1,2,0:T(8,128)(2,1)}, u32[]{:S(2)}, u32[]{:S(2)}) async-start(bf16[32,256,512]{1,2,0:T(8,128)(2,1)} %stack.3), calls=%async_computation | async-start | bytes 16777216 | tf_op jit(solution)/shard_map/all_to_all | solution.py:84
  50.8 1.5 fusion.82
  53.3 117.9 %all-to-all-done = bf16[32,256,512]{1,2,0:T(8,128)(2,1)} async-done(((bf16[32,256,512]{1,2,0:T(8,128)(2,1)}), bf16[32,256,512]{1,2,0:T(8,128)(2,1)}, u32[]{:S(2)}, u32[]{:S(2)}) %all-to-all-start) | async-done | bytes 8388640 | tf_op jit(solution)/shard_map/all_to_all | solution.py:84
  171.1 11.4 %copy.25 = bf16[32,256,512]{1,0,2:T(8,128)(2,1)} copy(bf16[32,256,512]{1,2,0:T(8,128)(2,1)} %all-to-all-done) | data formatting | bytes 16777216 | tf_op jit(solution)/shard_map/all_to_all | solution.py:84
  182.5 13.4 %reshape_reshape.3 = bf16[8192,4,128]{0,2,1:T(8,128)(2,1)} reshape(bf16[32,256,512]{1,0,2:T(8,128)(2,1)} %copy.25) | data formatting | bytes 16777216 | tf_op jit(solution)/shard_map/reshape;reshape | solution.py:89
  196.0 16.5 %fusion.101 = (f32[4,256]{1,0:T(4,128)S(1)}, f32[4,256,8192]{2,1,0:T(8,128)}) fusion(bf16[8192,4,128]{0,2,1:T(8,128)(2,1)} %reshape_reshape.3, bf16[256,4,128]{2,1,0:T(4,128)(2,1)S(1)} %multiply_convert_fusion), kind=kOutput, calls=%fused_computation.100 | convolution fusion | flops 2155871232 | bytes 42209280 | tf_op jit(solution)/shard_map/thd,shd->hts/dot_general | solution.py:36
  212.5 13.6 %fusion = f32[4,256]{1,0:T(4,128)S(1)} fusion(f32[4,256,8192]{2,1,0:T(8,128)} %get-tuple-element.10, f32[4,256]{1,0:T(4,128)S(1)} %broadcast_maximum_fusion), kind=kLoop, calls=%fused_computation.1 | loop fusion | flops 16776192 | bytes 33562624 | tf_op jit(solution)/shard_map/reduce_sum | solution.py:39
  226.2 12.0 %copy.30 = bf16[8192,512]{0,1:T(8,128)(2,1)} copy(bf16[8192,512]{1,0:T(8,128)(2,1)} %all-gather.2.cloned.1.call-done) | data formatting | bytes 16777216 | tf_op jit(solution)/shard_map/reshape | solution.py:90
  238.2 16.0 %fusion.45 = bf16[256,4,128]{0,2,1:T(8,128)(2,1)S(1)} fusion(bf16[8192,4,128]{0,2,1:T(8,128)(2,1)} %bitcast.66, f32[4,256,8192]{2,1,0:T(8,128)} %get-tuple-element.10, f32[4,256]{1,0:T(4,128)S(1)} %broadcast_maximum_fusion, f32[256,4]{0,1:T(4,128)S(1)} %bitcast.71), kind=kOutput, calls=%fused_computation.36 | convolution fusion | flops 2164523008 | bytes 42213376 | tf_op jit(solution)/shard_map/hts,shd->htd/dot_general | solution.py:40
  254.3 1.1 fusion.38
  (42 shorter events, 5.2 us)
Async XLA Ops:
  6.5 247.7 %copy-start = (bf16[512,768]{1,0:T(8,128)(2,1)S(1)}, bf16[512,768]{1,0:T(8,128)(2,1)}, u32[]{:S(2)}) copy-start(bf16[512,768]{1,0:T(8,128)(2,1)} %param.10) | copy-start | bytes 2359300
  6.5 219.6 %all-gather.2.cloned.1.call-start = ((), (), s32[]{:S(2)}) async-start(), calls=%async_computation.1 | async-start | bytes 8650752 | tf_op jit(solution)/shard_map/all_gather | solution.py:86
  7.4 8.7 %collective-permute-start.1 = (bf16[2,1536]{1,0:T(2,128)(2,1)S(1)}, bf16[2,1536]{1,0:T(2,128)(2,1)S(1)}, u32[]{:S(2)}, u32[]{:S(2)}) collective-permute-start(bf16[2,1536]{1,0:T(2,128)(2,1)S(1)} %get-tuple-element.6), channel_id=1, source_target_pairs={{4,0},{8,4},{12,8},{16,12},{20,16},{24,20},{28,24},{32,28},{36,32}... | collective-permute-start | bytes 18440 | tf_op jit(solution)/shard_map/ppermute | solution.py:16
  8.7 9.9 %copy-start.3 = (bf16[5,1536,768]{2,1,0:T(8,128)(2,1)S(1)}, bf16[5,1536,768]{2,1,0:T(8,128)(2,1)}, u32[]{:S(2)}) copy-start(bf16[5,1536,768]{2,1,0:T(8,128)(2,1)} %param.7) | copy-start | bytes 35389444
  8.7 10.7 %collective-permute-start = (bf16[2,1536]{1,0:T(2,128)(2,1)S(1)}, bf16[2,1536]{1,0:T(2,128)(2,1)S(1)}, u32[]{:S(2)}, u32[]{:S(2)}) collective-permute-start(bf16[2,1536]{1,0:T(2,128)(2,1)S(1)} %get-tuple-element.5), channel_id=1, source_target_pairs={{0,4},{4,8},{8,12},{12,16},{16,20},{20,24},{24,28},{28,32},{32,36}... | collective-permute-start | bytes 18440 | tf_op jit(solution)/shard_map/ppermute | solution.py:13
  16.0 3.4 %copy-start.2 = (bf16[256,1536]{1,0:T(8,128)(2,1)S(1)}, bf16[256,1536]{1,0:T(8,128)(2,1)}, u32[]{:S(2)}) copy-start(bf16[256,1536]{1,0:T(8,128)(2,1)} %param.6) | copy-start | bytes 2359300
  19.4 5.0 %slice-start = ((s8[5898240]{0:T(1024)(128)(4,1)}), s8[4194304]{0:T(1024)(128)(4,1)S(1)}, s32[]{:S(2)}) async-start(s8[5898240]{0:T(1024)(128)(4,1)} %bitcast.67), calls=%async_computation.2 | async-start | bytes 8388608
  20.2 4.2 %slice-start.1 = ((s8[5898240]{0:T(1024)(128)(4,1)}), s8[1703936]{0:T(1024)(128)(4,1)S(1)}, s32[]{:S(2)}) async-start(s8[5898240]{0:T(1024)(128)(4,1)} %bitcast.67), calls=%async_computation.3 | async-start | bytes 3407872
  21.3 4.9 %collective-permute-start.2 = (bf16[2,768]{1,0:T(2,128)(2,1)S(1)}, bf16[2,768]{1,0:T(2,128)(2,1)S(1)}, u32[]{:S(2)}, u32[]{:S(2)}) collective-permute-start(bf16[2,768]{1,0:T(2,128)(2,1)S(1)} %get-tuple-element.7), channel_id=1, source_target_pairs={{0,4},{4,8},{8,12},{12,16},{16,20},{20,24},{24,28},{28,32},{32,36}... | collective-permute-start | bytes 9224 | tf_op jit(solution)/shard_map/ppermute | solution.py:13
  24.9 3.6 %collective-permute-start.3 = (bf16[2,768]{1,0:T(2,128)(2,1)S(1)}, bf16[2,768]{1,0:T(2,128)(2,1)S(1)}, u32[]{:S(2)}, u32[]{:S(2)}) collective-permute-start(bf16[2,768]{1,0:T(2,128)(2,1)S(1)} %get-tuple-element.8), channel_id=1, source_target_pairs={{4,0},{8,4},{12,8},{16,12},{20,16},{24,20},{28,24},{32,28},{36,32}... | collective-permute-start | bytes 9224 | tf_op jit(solution)/shard_map/ppermute | solution.py:16
  26.7 3.3 %copy-start.1 = (bf16[768,1536]{1,0:T(8,128)(2,1)S(1)}, bf16[768,1536]{1,0:T(8,128)(2,1)}, u32[]{:S(2)}) copy-start(bf16[768,1536]{1,0:T(8,128)(2,1)} %param.9) | copy-start | bytes 7077892
  36.7 14.1 %copy-start.4 = (f32[4]{0:T(128)S(1)}, f32[4]{0:T(128)}, u32[]{:S(2)}) copy-start(f32[4]{0:T(128)} %param.11) | copy-start | bytes 52
  36.7 134.4 %all-to-all-start = ((bf16[32,256,512]{1,2,0:T(8,128)(2,1)}), bf16[32,256,512]{1,2,0:T(8,128)(2,1)}, u32[]{:S(2)}, u32[]{:S(2)}) async-start(bf16[32,256,512]{1,2,0:T(8,128)(2,1)} %stack.3), calls=%async_computation | async-start | bytes 16777216 | tf_op jit(solution)/shard_map/all_to_all | solution.py:84
Sparse Core Ops, SparseCore 0:
  31.5 135.2 all-gather.1
